TPU v7x, 256 devices: a whole 4x4x8 slice. The times are simulated.
256 devices in a mesh: ctx: 32 (over y, z), ret: 2 (over core), tp: 4 (over x).
Axes of the slice: x: 4, y: 4, z: 8, core: 2. Of those that a mesh axis runs over, the one named last changes fastest.
Arguments:
- queries: bfloat16 [32768, 2048], P('ctx', 'tp'), may hold values from -256 to 256
- d_attn: bfloat16 [32768, 2048], P('ctx', 'tp'), may hold values from -6 to 6
- pool: bfloat16 [2, 32768, 896], P('ret', 'ctx'), may hold values from -6 to 6
- w_key: bfloat16 [896, 2048], P(None, 'tp'), may hold values from -0.1875 to 0.1875
- w_value: bfloat16 [896, 2048], P(None, 'tp'), may hold values from -0.1875 to 0.1875
- owners: int32 [512, 2], replicated, may hold values from 0 to 31, as said below
- picks: int32 [512, 2], replicated, may hold values from 0 to 1023
- live_counts: int32 [2, 32], replicated, may hold values from 1 to 8
Outputs:
- attn_out: bfloat16 [32768, 2048], P('ctx', 'tp')
- d_queries: bfloat16 [32768, 2048], P('ctx', 'tp')
- d_w_key: bfloat16 [896, 2048], P(None, 'tp')
- d_w_value: bfloat16 [896, 2048], P(None, 'tp')
Inputs may be any that keep to these rules, and one draw needn't show every extreme that they name: `owners`: in each column, at most 1 of the 16 spans of one ctx slab name the same owner, and in every slab some owner is named exactly 1 times.
All inputs are finite; a program needn't handle non-finite values.
Results may differ from a plain program's by a relative error of at most 0.0095.
The roundings to bfloat16 on the way count: a program that leaves them out, or rounds other values in their place, can miss the bound.
Values may be sent and summed in bfloat16 or wider, within the bound.
No kernel may reach another device: no remote copies, remote signals or barrier semaphores. Data moves between devices by JAX's collectives and lax.ppermute only.
A program may use at most 128 MiB of HBM per device.

v0:
```python
import math
import jax
import jax.numpy as jnp
from jax import lax
from jax.sharding import PartitionSpec as P

HEAD_DIM = 128
SPAN = 64
NBR_LEN = 128
CH_DEV = 16


def combined_all(x, axis, combine):
    everything = jax.tree.map(lambda part: lax.all_gather(part, axis), x)
    leading = jax.tree.map(lambda part: part[0], everything)

    def hop(k, so_far):
        return combine(so_far, jax.tree.map(lambda part: part[k], everything))

    return lax.fori_loop(1, lax.axis_size(axis), hop, leading)


def combine_stats(earlier, later):
    first_max, first_total = earlier
    second_max, second_total = later
    joint_max = jnp.maximum(first_max, second_max)
    joint_total = first_total * jnp.exp(first_max - joint_max) + second_total * jnp.exp(
        second_max - joint_max
    )
    return (joint_max, joint_total)


def body(queries, d_attn, pool, w_key, w_value, owners, picks, live_counts):
    ctx_count = lax.axis_size("ctx")
    ctx_place = lax.axis_index("ctx")
    ret_place = lax.axis_index("ret")
    capacity = (CH_DEV + ctx_count - 1) // ctx_count
    head_cols = w_key.shape[1]
    local_heads = head_cols // HEAD_DIM
    blocks = pool.shape[1] // NBR_LEN
    enc_width = pool.shape[2]
    score_scale = 1.0 / math.sqrt(HEAD_DIM)
    owner_col = lax.dynamic_index_in_dim(owners, ret_place, 1, keepdims=False)
    pick_col = lax.dynamic_index_in_dim(picks, ret_place, 1, keepdims=False)
    count_row = lax.dynamic_index_in_dim(live_counts, ret_place, 0, keepdims=False)
    owner_ids = jnp.arange(ctx_count, dtype=jnp.int32)
    counts_of = jnp.sum(
        jnp.where(owner_col[:, None] == owner_ids[None, :], count_row[None, :], 0), axis=1
    )
    slot_col = pick_col % counts_of
    owner_grid = owner_col.reshape(ctx_count, CH_DEV)
    slot_grid = slot_col.reshape(ctx_count, CH_DEV)
    position = jnp.arange(CH_DEV, dtype=jnp.int32)
    earlier = position[None, :] < position[:, None]
    same_owner = owner_grid[:, :, None] == owner_grid[:, None, :]
    request_rank = jnp.sum(jnp.logical_and(same_owner, earlier[None]), axis=2)
    places = jnp.arange(capacity, dtype=jnp.int32)
    wanted = jnp.logical_and(
        (owner_grid == ctx_place)[:, None, :], request_rank[:, None, :] == places[None, :, None]
    )
    send_slot = jnp.sum(jnp.where(wanted, slot_grid[:, None, :], 0), axis=2).reshape(-1)
    send_live = jnp.any(wanted, axis=2).reshape(-1)
    my_owner = lax.dynamic_index_in_dim(owner_grid, ctx_place, 0, keepdims=False)
    my_rank = lax.dynamic_index_in_dim(request_rank, ctx_place, 0, keepdims=False)
    recv_index = my_owner * capacity + my_rank
    pool_blocks = pool[0].reshape(blocks, NBR_LEN, enc_width)
    flat_pool = pool[0]
    own_keys = jnp.dot(flat_pool, w_key, preferred_element_type=jnp.float32).astype(jnp.bfloat16)
    own_values = jnp.dot(flat_pool, w_value, preferred_element_type=jnp.float32).astype(
        jnp.bfloat16
    )
    own_pair = jnp.concatenate([own_keys, own_values], axis=1).reshape(
        blocks, NBR_LEN, 2 * head_cols
    )
    outgoing = jnp.take(own_pair, send_slot, axis=0)
    incoming = lax.all_to_all(outgoing, "ctx", split_axis=0, concat_axis=0, tiled=True)
    chosen = jnp.take(incoming, recv_index, axis=0)
    key_tiles = chosen[:, :, :head_cols]
    value_tiles = chosen[:, :, head_cols:]
    query_tiles = queries.reshape(CH_DEV, SPAN, local_heads, HEAD_DIM)
    grad_out = d_attn.reshape(CH_DEV, SPAN, local_heads, HEAD_DIM)
    key_four = key_tiles.reshape(CH_DEV, NBR_LEN, local_heads, HEAD_DIM)
    value_four = value_tiles.reshape(CH_DEV, NBR_LEN, local_heads, HEAD_DIM)
    scores = (
        jnp.einsum("cmhd,clhd->chml", query_tiles, key_four, preferred_element_type=jnp.float32)
        * score_scale
    )
    local_max = jnp.max(scores, axis=3)
    local_total = jnp.sum(jnp.exp(scores - local_max[..., None]), axis=3)
    row_max, row_total = combined_all((local_max, local_total), "ret", combine_stats)
    attn_prob = jnp.exp(scores - row_max[..., None]) / row_total[..., None]
    prob_bf = attn_prob.astype(jnp.bfloat16)
    partial_value = jnp.einsum(
        "chml,clhd->cmhd", prob_bf, value_four, preferred_element_type=jnp.float32
    )
    attn_full = lax.psum(partial_value.reshape(CH_DEV * SPAN, head_cols), "ret")
    attn_out = attn_full.astype(jnp.bfloat16)
    out_dot = jnp.sum(
        grad_out.astype(jnp.float32)
        * attn_out.reshape(CH_DEV, SPAN, local_heads, HEAD_DIM).astype(jnp.float32),
        axis=3,
    )
    out_dot = jnp.transpose(out_dot, (0, 2, 1))
    grad_prob = jnp.einsum(
        "cmhd,clhd->chml", grad_out, value_four, preferred_element_type=jnp.float32
    )
    dscore = (attn_prob * (grad_prob - out_dot[..., None]) * score_scale).astype(jnp.bfloat16)
    dq_part = jnp.einsum("chml,clhd->cmhd", dscore, key_four, preferred_element_type=jnp.float32)
    d_queries = lax.psum(dq_part.reshape(CH_DEV * SPAN, head_cols), "ret").astype(jnp.bfloat16)
    key_grad = jnp.einsum(
        "chml,cmhd->clhd", dscore, query_tiles, preferred_element_type=jnp.float32
    ).astype(jnp.bfloat16)
    value_grad = jnp.einsum(
        "chml,cmhd->clhd", prob_bf, grad_out, preferred_element_type=jnp.float32
    ).astype(jnp.bfloat16)
    grad_pair = jnp.concatenate(
        [
            key_grad.reshape(CH_DEV, NBR_LEN, head_cols),
            value_grad.reshape(CH_DEV, NBR_LEN, head_cols),
        ],
        axis=2,
    )
    mean_share = 1.0 / (CH_DEV * ctx_count)
    back_hit = recv_index[None, :] == jnp.arange(ctx_count * capacity, dtype=jnp.int32)[:, None]
    back_span = jnp.sum(jnp.where(back_hit, position[None, :], 0), axis=1)
    returning = jnp.take(grad_pair, back_span, axis=0)
    arrived = lax.all_to_all(returning, "ctx", split_axis=0, concat_axis=0, tiled=True)
    arrived = arrived * send_live[:, None, None].astype(jnp.bfloat16)
    source = jnp.take(pool_blocks, send_slot, axis=0).reshape(-1, enc_width)
    weight_part = (
        jnp.einsum(
            "re,rk->ek",
            source,
            arrived.reshape(-1, 2 * head_cols),
            preferred_element_type=jnp.float32,
        )
        * mean_share
    )
    weight_sum = lax.psum(weight_part, ("ctx", "ret"))
    d_w_key = weight_sum[:, :head_cols].astype(jnp.bfloat16)
    d_w_value = weight_sum[:, head_cols:].astype(jnp.bfloat16)
    return (attn_out, d_queries, d_w_key, d_w_value)


def solution(mesh):
    return jax.shard_map(
        body,
        mesh=mesh,
        in_specs=(
            P("ctx", "tp"),
            P("ctx", "tp"),
            P("ret", "ctx", None),
            P(None, "tp"),
            P(None, "tp"),
            P(),
            P(),
            P(),
        ),
        out_specs=(P("ctx", "tp"), P("ctx", "tp"), P(None, "tp"), P(None, "tp")),
        check_vma=False,
    )
```

profile of v0, /device:TPU:2, one launch (start us, length us, event | category | flops | bytes accessed | tf_op | source)
XLA Modules:
  0.0 822.3 jit_solution(8104515446239602236)
XLA Ops:
  0.6 0.0 copy-start
  0.7 0.8 fusion.36
  1.5 0.7 dynamic-slice_reduce_fusion
  2.2 0.5 broadcast.249
  2.7 1.4 fusion.44
  4.1 0.1 eq.121
  4.2 0.1 copy.76
  4.3 0.1 select_reduce_fusion
  4.3 0.1 reduce_sum.62
  4.4 0.1 copy.77
  4.5 0.1 reshape.285
  4.6 0.1 copy.73
  4.6 0.1 convert_reduce_fusion
  4.8 0.2 add_reduce_fusion
  5.0 0.1 select_reduce_fusion.1
  5.1 0.1 squeeze.27
  5.2 0.1 copy.79
  5.2 0.2 fusion.35
  5.4 0.0 copy-start.6
  5.5 2.5 fusion.20
  8.0 1.3 fusion.23
  9.3 1.5 pad_maximum_fusion.1
  10.8 4.0 copy.102
  14.8 6.5 gather_fusion
  21.3 7.5 broadcast_select_fusion.1
  28.8 11.7 %all-to-all-start = ((bf16[32,128,1024]{2,1,0:T(8,128)(2,1)}), bf16[32,128,1024]{2,1,0:T(8,128)(2,1)}, u32[]{:S(2)}, u32[]{:S(2)}) async-start(bf16[32,128,1024]{2,1,0:T(8,128)(2,1)} %broadcast_select_fusion.1), calls=%async_computation | async-start | bytes 16777216 | tf_op jit(solution)/shard_map/all_to_all | solution.py:76
  40.5 1.1 reshape.291
  41.6 1.3 reshape.289
  43.0 184.8 %all-to-all-done = bf16[32,128,1024]{2,1,0:T(8,128)(2,1)} async-done(((bf16[32,128,1024]{2,1,0:T(8,128)(2,1)}), bf16[32,128,1024]{2,1,0:T(8,128)(2,1)}, u32[]{:S(2)}, u32[]{:S(2)}) %all-to-all-start) | async-done | bytes 8388640 | tf_op jit(solution)/shard_map/all_to_all | solution.py:76
  227.8 6.2 gather_fusion.1
  234.0 2.6 broadcast_select_fusion.2
  236.6 2.5 fusion.45
  239.2 4.0 copy.82
  243.1 3.9 copy.81
  247.1 2.4 bitcast_reduce_fusion
  249.5 0.0 copy-start.2
  249.5 2.0 all-gather
  251.4 1.3 fusion.15
  252.8 2.0 all-gather.1
  254.9 3.1 convolution_convert_fusion
  258.0 3.9 copy.95
  261.9 3.0 convolution_bitcast_fusion.1
  264.9 1.4 copy.86
  266.3 1.5 copy.118
  267.8 9.9 %all-reduce.3 = bf16[1024,512]{1,0:T(8,128)(2,1)} all-reduce(f32[1024,512]{1,0:T(8,128)} %bitcast.94), channel_id=1, replica_groups=mesh['ctx'=32,'ret'=2,'tp'=4] {'ret'}, use_global_device_ids=true, to_apply=%region_5.6 | all-reduce | flops 524288 | bytes 3145728 | tf_op jit(solution)/shard_map/psum | solution.py:96
  277.7 2.7 reshape.295
  280.5 3.0 multiply_reduce_fusion
  283.5 0.2 copy.89
  283.7 4.0 fusion.11
  287.7 2.1 convolution_convert_fusion.1
  289.8 3.9 copy.94
  293.8 4.8 pad_maximum_fusion
  298.5 7.1 gather_fusion.3
  305.6 7.5 broadcast_select_fusion
  313.1 13.5 %all-to-all-start.1 = ((bf16[32,128,1024]{2,1,0:T(8,128)(2,1)}), bf16[32,128,1024]{2,1,0:T(8,128)(2,1)}, u32[]{:S(2)}, u32[]{:S(2)}) async-start(bf16[32,128,1024]{2,1,0:T(8,128)(2,1)} %broadcast_select_fusion), calls=%async_computation.1 | async-start | bytes 16777216 | tf_op jit(solution)/shard_map/all_to_all | solution.py:127
  326.6 4.4 gather_fusion.2
  330.9 3.1 convolution_bitcast_fusion
  334.1 1.4 copy.91
  335.5 1.6 copy.117
  337.0 9.9 %all-reduce.4 = bf16[1024,512]{1,0:T(8,128)(2,1)} all-reduce(f32[1024,512]{1,0:T(8,128)} %bitcast.97), channel_id=1, replica_groups=mesh['ctx'=32,'ret'=2,'tp'=4] {'ret'}, use_global_device_ids=true, to_apply=%region_7.8 | all-reduce | flops 524288 | bytes 3145728 | tf_op jit(solution)/shard_map/psum | solution.py:109
  346.9 169.6 %all-to-all-done.1 = bf16[32,128,1024]{2,1,0:T(8,128)(2,1)} async-done(((bf16[32,128,1024]{2,1,0:T(8,128)(2,1)}), bf16[32,128,1024]{2,1,0:T(8,128)(2,1)}, u32[]{:S(2)}, u32[]{:S(2)}) %all-to-all-start.1) | async-done | bytes 8388640 | tf_op jit(solution)/shard_map/all_to_all | solution.py:127
  516.5 13.8 %bitcast_multiply_fusion = f32[896,1024]{1,0:T(8,128)} fusion(bf16[32,128,1024]{2,1,0:T(8,128)(2,1)} %all-to-all-done.1, bf16[32]{0:T(256)(128)(2,1)S(1)} %convert_element_type.66, bf16[32,128,896]{2,1,0:T(8,128)(2,1)} %gather_fusion.2, pred[32]{0:T(512)(128)(4,1)S(1)} %get-tuple-element.35), kind=kOutput, calls=%fused_computation.13 | convolution fusion | flops 7524974592 | bytes 19398752 | tf_op jit(solution)/shard_map/re,rk->ek/dot_general | solution.py:131
  530.3 289.2 %all-reduce.5 = bf16[896,1024]{1,0:T(8,128)(2,1)} all-reduce(f32[896,1024]{1,0:T(8,128)} %bitcast_multiply_fusion), channel_id=1, replica_groups=mesh['ctx'=32,'ret'=2,'tp'=4] {'ctx','ret'}, use_global_device_ids=true, to_apply=%region_10.11 | all-reduce | flops 917504 | bytes 5505024 | tf_op jit(solution)/shard_map/psum | solution.py:139
  819.5 2.8 fusion.46
  (23 shorter events, 0.2 us)
Async XLA Ops:
  0.6 4.8 copy-start
  5.4 2.6 copy-start.6
  28.7 11.7 %copy-start.5 = (bf16[1024,512]{1,0:T(8,128)(2,1)S(1)}, bf16[1024,512]{1,0:T(8,128)(2,1)}, u32[]{:S(2)}) copy-start(bf16[1024,512]{1,0:T(8,128)(2,1)} %param.9) | copy-start | bytes 3145732
  28.8 199.1 %all-to-all-start = ((bf16[32,128,1024]{2,1,0:T(8,128)(2,1)}), bf16[32,128,1024]{2,1,0:T(8,128)(2,1)}, u32[]{:S(2)}, u32[]{:S(2)}) async-start(bf16[32,128,1024]{2,1,0:T(8,128)(2,1)} %broadcast_select_fusion.1), calls=%async_computation | async-start | bytes 16777216 | tf_op jit(solution)/shard_map/all_to_all | solution.py:76
  249.4 8.5 %copy-start.1 = (f32[16,4,128,64]{2,3,1,0:T(8,128)}, f32[16,4,128,64]{2,3,1,0:T(8,128)S(1)}, u32[]{:S(2)}) copy-start(f32[16,4,128,64]{2,3,1,0:T(8,128)S(1)} %get-tuple-element.33) | copy-start | bytes 6291460
  249.5 5.4 copy-start.2
  287.7 2.1 copy-start.3
  313.1 203.5 %all-to-all-start.1 = ((bf16[32,128,1024]{2,1,0:T(8,128)(2,1)}), bf16[32,128,1024]{2,1,0:T(8,128)(2,1)}, u32[]{:S(2)}, u32[]{:S(2)}) async-start(bf16[32,128,1024]{2,1,0:T(8,128)(2,1)} %broadcast_select_fusion), calls=%async_computation.1 | async-start | bytes 16777216 | tf_op jit(solution)/shard_map/all_to_all | solution.py:127
  326.6 4.4 copy-start.4
where the time goes:
time: 823 us; the launch traced here: 822 us
  waiting for transfers between devices  354 us (43%)
  blocking collectives  313 us (38%)
  local copies, waits for them, and re-layouts  64.5 us (8%)
  matrix products  35.3 us (4%)
  other arithmetic  28.9 us (4%)
  starting transfers between devices  25.2 us (3%)
    psum x1, blocking collectives, body(): weight_sum = lax.psum(weight_part, ('ctx', 'ret'))  289 us
    all_to_all x1, waiting for transfers between devices, body(): lax.all_to_all(outgoing, 'ctx', split_axis=0, concat_axis=0, tiled=True)  185 us
    all_to_all x1, waiting for transfers between devices, body(): lax.all_to_all(returning, 'ctx', split_axis=0, concat_axis=0, tiled=True)  170 us
  transfers between devices with their start and end apart: 2, of which 2 were waited for; matrix products, arithmetic and copies ran while one was open for 2% of the time, Pallas kernels for 0%

commit v1 on v0

--- a/solution.py
+++ b/solution.py
@@ -136,7 +136,7 @@
         )
         * mean_share
     )
-    weight_sum = lax.psum(weight_part, ("ctx", "ret"))
+    weight_sum = lax.psum(lax.psum(weight_part, "ret"), "ctx")
     d_w_key = weight_sum[:, :head_cols].astype(jnp.bfloat16)
     d_w_value = weight_sum[:, head_cols:].astype(jnp.bfloat16)
     return (attn_out, d_queries, d_w_key, d_w_value)

time: 823 us -> 765 us (0.930)
  blocking collectives: 313 us -> 201 us
  waiting for transfers between devices: 354 us -> 393 us
  between operations: 0.92 us -> 14.3 us
    psum x1, blocking collectives: 289 us -> 177 us  [body(): weight_sum = lax.psum(lax.psum(weight_part, 'ret'), 'ctx')]
    psum x0 -> x1, waiting for transfers between devices: none -> 22.4 us  [body(): weight_sum = lax.psum(lax.psum(weight_part, 'ret'), 'ctx')]
    all_to_all x1, waiting for transfers between devices: 170 us -> 186 us  [body(): lax.all_to_all(returning, 'ctx', split_axis=0, concat_axis=0, tiled=True)]
  transfers between devices with their start and end apart: 2 -> 3, of which waited for: 2 -> 3; matrix products, arithmetic and copies ran while one was open for 2% -> 2% of each run, Pallas kernels for 0% -> 0%
where the time goes in v1:
time: 765 us; the launch traced here: 764 us
  waiting for transfers between devices  393 us (51%)
  blocking collectives  201 us (26%)
  local copies, waits for them, and re-layouts  65.6 us (9%)
  matrix products  35.3 us (5%)
  other arithmetic  28.9 us (4%)
  starting transfers between devices  25.3 us (3%)
  between operations  14.3 us (2%)
    all_to_all x1, waiting for transfers between devices, body(): lax.all_to_all(returning, 'ctx', split_axis=0, concat_axis=0, tiled=True)  186 us
    all_to_all x1, waiting for transfers between devices, body(): lax.all_to_all(outgoing, 'ctx', split_axis=0, concat_axis=0, tiled=True)  185 us
    psum x1, blocking collectives, body(): weight_sum = lax.psum(lax.psum(weight_part, 'ret'), 'ctx')  177 us
    psum x1, waiting for transfers between devices, body(): weight_sum = lax.psum(lax.psum(weight_part, 'ret'), 'ctx')  22.4 us
  transfers between devices with their start and end apart: 3, of which 3 were waited for; matrix products, arithmetic and copies ran while one was open for 2% of the time, Pallas kernels for 0%

profile of v1, /device:TPU:2, one launch (start us, length us, event | category | flops | bytes accessed | tf_op | source)
XLA Modules:
  0.0 763.6 jit_solution(15549320527762230271)
XLA Ops:
  7.2 0.8 fusion.36
  8.0 0.7 dynamic-slice_reduce_fusion
  8.7 0.5 broadcast.249
  9.2 1.4 fusion.44
  10.6 0.1 eq.121
  10.7 0.1 copy.76
  10.8 0.1 select_reduce_fusion
  10.9 0.1 reduce_sum.62
  11.0 0.1 copy.77
  11.0 0.1 reshape.285
  11.1 0.1 copy.73
  11.2 0.1 convert_reduce_fusion
  11.3 0.2 add_reduce_fusion
  11.5 0.1 select_reduce_fusion.1
  11.6 0.1 squeeze.27
  11.7 0.1 copy.79
  11.8 0.2 fusion.35
  12.0 2.5 fusion.20
  14.6 1.3 fusion.23
  15.9 1.5 pad_maximum_fusion.1
  17.3 4.0 copy.102
  21.3 6.5 gather_fusion
  27.8 7.5 broadcast_select_fusion.1
  35.3 11.7 %all-to-all-start = ((bf16[32,128,1024]{2,1,0:T(8,128)(2,1)}), bf16[32,128,1024]{2,1,0:T(8,128)(2,1)}, u32[]{:S(2)}, u32[]{:S(2)}) async-start(bf16[32,128,1024]{2,1,0:T(8,128)(2,1)} %broadcast_select_fusion.1), calls=%async_computation | async-start | bytes 16777216 | tf_op jit(solution)/shard_map/all_to_all | solution.py:76
  47.0 1.1 reshape.291
  48.1 1.3 reshape.289
  49.5 184.8 %all-to-all-done = bf16[32,128,1024]{2,1,0:T(8,128)(2,1)} async-done(((bf16[32,128,1024]{2,1,0:T(8,128)(2,1)}), bf16[32,128,1024]{2,1,0:T(8,128)(2,1)}, u32[]{:S(2)}, u32[]{:S(2)}) %all-to-all-start) | async-done | bytes 8388640 | tf_op jit(solution)/shard_map/all_to_all | solution.py:76
  234.4 6.2 gather_fusion.1
  240.5 2.6 broadcast_select_fusion.2
  243.2 2.5 fusion.45
  245.7 4.0 copy.82
  249.7 3.9 copy.81
  253.6 2.4 bitcast_reduce_fusion
  256.0 2.0 all-gather
  258.0 1.3 fusion.15
  259.3 2.0 all-gather.1
  261.4 3.1 convolution_convert_fusion
  264.5 3.9 copy.95
  268.4 3.0 convolution_bitcast_fusion.1
  271.4 1.4 copy.86
  272.9 1.5 copy.118
  274.4 9.9 %all-reduce.6 = bf16[1024,512]{1,0:T(8,128)(2,1)} all-reduce(f32[1024,512]{1,0:T(8,128)} %bitcast.94), channel_id=1, replica_groups=mesh['ctx'=32,'ret'=2,'tp'=4] {'ret'}, use_global_device_ids=true, to_apply=%region_5.6 | all-reduce | flops 524288 | bytes 3145728 | tf_op jit(solution)/shard_map/psum | solution.py:96
  284.3 2.7 reshape.295
  287.0 3.0 multiply_reduce_fusion
  290.0 0.2 copy.89
  290.2 4.0 fusion.11
  294.2 2.1 convolution_convert_fusion.1
  296.4 3.9 copy.94
  300.3 4.8 pad_maximum_fusion
  305.0 7.1 gather_fusion.3
  312.1 7.5 broadcast_select_fusion
  319.6 13.3 %all-to-all-start.1 = ((bf16[32,128,1024]{2,1,0:T(8,128)(2,1)}), bf16[32,128,1024]{2,1,0:T(8,128)(2,1)}, u32[]{:S(2)}, u32[]{:S(2)}) async-start(bf16[32,128,1024]{2,1,0:T(8,128)(2,1)} %broadcast_select_fusion), calls=%async_computation.1 | async-start | bytes 16777216 | tf_op jit(solution)/shard_map/all_to_all | solution.py:127
  332.9 0.3 all-reduce.5.cloned.1.call-start
  333.2 4.4 gather_fusion.2
  337.5 186.2 %all-to-all-done.1 = bf16[32,128,1024]{2,1,0:T(8,128)(2,1)} async-done(((bf16[32,128,1024]{2,1,0:T(8,128)(2,1)}), bf16[32,128,1024]{2,1,0:T(8,128)(2,1)}, u32[]{:S(2)}, u32[]{:S(2)}) %all-to-all-start.1) | async-done | bytes 8388640 | tf_op jit(solution)/shard_map/all_to_all | solution.py:127
  523.7 13.8 %bitcast_multiply_fusion = f32[896,1024]{1,0:T(8,128)} fusion(bf16[32,128,1024]{2,1,0:T(8,128)(2,1)} %all-to-all-done.1, bf16[32]{0:T(256)(128)(2,1)S(1)} %convert_element_type.66, bf16[32,128,896]{2,1,0:T(8,128)(2,1)} %gather_fusion.2, pred[32]{0:T(512)(128)(4,1)S(1)} %get-tuple-element.35), kind=kOutput, calls=%fused_computation.13 | convolution fusion | flops 7524974592 | bytes 19398752 | tf_op jit(solution)/shard_map/re,rk->ek/dot_general | solution.py:131
  537.5 1.2 copy-done.4
  538.7 3.1 convolution_bitcast_fusion
  541.8 1.4 copy.91
  543.2 1.5 copy.117
  544.7 9.9 %all-reduce.7 = bf16[1024,512]{1,0:T(8,128)(2,1)} all-reduce(f32[1024,512]{1,0:T(8,128)} %bitcast.97), channel_id=1, replica_groups=mesh['ctx'=32,'ret'=2,'tp'=4] {'ret'}, use_global_device_ids=true, to_apply=%region_7.8 | all-reduce | flops 524288 | bytes 3145728 | tf_op jit(solution)/shard_map/psum | solution.py:109
  554.6 22.4 %all-reduce.5.cloned.1.call-done = f32[896,1024]{1,0:T(8,128)} async-done(((f32[896,1024]{1,0:T(8,128)}), f32[896,1024]{1,0:T(8,128)}) %all-reduce.5.cloned.1.call-update) | async-done | bytes 3670032 | tf_op jit(solution)/shard_map/psum | solution.py:139
  577.0 177.0 %all-reduce.8 = bf16[896,1024]{1,0:T(8,128)(2,1)} all-reduce(f32[896,1024]{1,0:T(8,128)} %all-reduce.5.cloned.1.call-done), channel_id=1, replica_groups=mesh['ctx'=32,'ret'=2,'tp'=4] {'ctx'}, use_global_device_ids=true, to_apply=%region_11.12 | all-reduce | flops 917504 | bytes 5505024 | tf_op jit(solution)/shard_map/psum | solution.py:139
  754.0 2.8 fusion.46
  (26 shorter events, 0.2 us)
Async XLA Ops:
  7.2 4.8 copy-start
  12.0 2.6 copy-start.6
  35.3 11.7 %copy-start.5 = (bf16[1024,512]{1,0:T(8,128)(2,1)S(1)}, bf16[1024,512]{1,0:T(8,128)(2,1)}, u32[]{:S(2)}) copy-start(bf16[1024,512]{1,0:T(8,128)(2,1)} %param.9) | copy-start | bytes 3145732
  35.3 199.1 %all-to-all-start = ((bf16[32,128,1024]{2,1,0:T(8,128)(2,1)}), bf16[32,128,1024]{2,1,0:T(8,128)(2,1)}, u32[]{:S(2)}, u32[]{:S(2)}) async-start(bf16[32,128,1024]{2,1,0:T(8,128)(2,1)} %broadcast_select_fusion.1), calls=%async_computation | async-start | bytes 16777216 | tf_op jit(solution)/shard_map/all_to_all | solution.py:76
  256.0 8.5 %copy-start.1 = (f32[16,4,128,64]{2,3,1,0:T(8,128)}, f32[16,4,128,64]{2,3,1,0:T(8,128)S(1)}, u32[]{:S(2)}) copy-start(f32[16,4,128,64]{2,3,1,0:T(8,128)S(1)} %get-tuple-element.33) | copy-start | bytes 6291460
  256.0 5.4 copy-start.2
  294.2 2.1 copy-start.3
  319.6 204.1 %all-to-all-start.1 = ((bf16[32,128,1024]{2,1,0:T(8,128)(2,1)}), bf16[32,128,1024]{2,1,0:T(8,128)(2,1)}, u32[]{:S(2)}, u32[]{:S(2)}) async-start(bf16[32,128,1024]{2,1,0:T(8,128)(2,1)} %broadcast_select_fusion), calls=%async_computation.1 | async-start | bytes 16777216 | tf_op jit(solution)/shard_map/all_to_all | solution.py:127
  332.9 244.1 %all-reduce.5.cloned.1.call-start = ((), (), s32[]{:S(2)}) async-start(), calls=%async_computation.2 | async-start | bytes 7340032 | tf_op jit(solution)/shard_map/psum | solution.py:139
  537.4 1.2 copy-start.4
Sparse Core Ops, SparseCore 0:
  537.6 39.3 all-reduce.4
